TPU v7x, 32 devices: a whole 2x2x4 slice. The times are simulated.
32 devices in a mesh: groups: 2 (over y), ctx: 4 (over z), exp: 2 (over x), tp: 2 (over core).
Axes of the slice: x: 2, y: 2, z: 4, core: 2. Of those that a mesh axis runs over, the one named last changes fastest.
Arguments:
- queries: bfloat16 [4, 512, 20, 128], P(('groups', 'exp'), 'ctx', 'tp'), parts along dimension 0, may hold values from -9 to 9
- key_states: bfloat16 [4, 512, 4, 128], P(('groups', 'exp'), 'ctx', 'tp'), parts along dimension 0, may hold values from -9 to 9
- values: bfloat16 [4, 512, 4, 128], P(('groups', 'exp'), 'ctx', 'tp'), parts along dimension 0, may hold values from -6 to 6
- doc_ids: int32 [4, 512], P(('groups', 'exp'), 'ctx'), parts along dimension 0, may hold values from 0 to 3, never falling along the last dimension, each value on 1 to 256 neighbouring positions
- residual: bfloat16 [4, 512, 5120], P(('groups', 'exp'), ('ctx', 'tp')), parts along dimension 0, may hold values from -6 to 6
- out_proj: bfloat16 [2560, 5120], P('tp', 'ctx'), may hold values from -0.125 to 0.125
- norm_gain: bfloat16 [5120], replicated, may hold values from 0.5 to 1.5
- router: bfloat16 [5120, 64], P(None, 'exp'), may hold values from -0.078125 to 0.078125
- expert_ids: int32 [4, 512, 1], P(('groups', 'exp'), ('ctx', 'tp')), parts along dimension 0, may hold values from 0 to 63; in each aligned block of 64 rows (0 to 63, 64 to 127, ..., all dimensions but the last counted through in order) at most 2 rows name the same one
- keep_counts: int32 [128], P('groups'), parts along dimension 0, may hold values from 1 to 2
Outputs:
- expert_inputs: bfloat16 [32, 64, 2, 5120], P(('groups', 'ctx', 'tp'), 'exp'), parts along dimension 0
There are 2 independent parts, one for each index of `groups`. A program takes and returns all parts, laid end to end along the dimension named above; an argument that names none is the same for every part. Nothing has to cross between parts.
Inputs may be any that keep to these rules, and one draw needn't show every extreme that they name: `doc_ids`: doc ids never fall along a request; a document holds at most 256 tokens, and some document holds exactly that many. `expert_ids`: in each aligned block of 64 tokens (the rows of one device) no expert is named more than 2 times, and in some blocks one expert is named exactly 2 times.
All inputs are finite; a program needn't handle non-finite values.
Results may differ from a plain program's by a relative error of at most 0.013.
Values may be sent and summed in bfloat16 or wider, within the bound.
A program may use at most 64 MiB of HBM per device.

v0:
```python
import math
import jax
import jax.numpy as jnp
from jax import lax
from jax.sharding import PartitionSpec as P

CAP = 2
EPSILON = 1e-05


def on_device(
    queries,
    key_states,
    values,
    doc_ids,
    residual,
    out_proj,
    norm_gain,
    router,
    expert_ids,
    keep_counts,
):
    tokens_here = queries.shape[1]
    heads_here = queries.shape[2]
    head_size = queries.shape[3]
    groups_here = key_states.shape[2]
    mixing_ratio = heads_here // groups_here
    ctx_count = lax.axis_size("ctx")
    pair_count = lax.axis_size("tp")
    part_rows = tokens_here // pair_count
    first_token = lax.axis_index("ctx") * tokens_here
    scale = 1.0 / math.sqrt(head_size)
    query_rows = (
        queries[0].reshape(tokens_here, groups_here, mixing_ratio, head_size).transpose(1, 0, 2, 3)
    )
    query_rows = query_rows.reshape(groups_here, tokens_here * mixing_ratio, head_size)
    query_place = (
        first_token
        + lax.broadcasted_iota(jnp.int32, (tokens_here * mixing_ratio,), 0) // mixing_ratio
    )
    query_docs = jnp.repeat(doc_ids[0], mixing_ratio)

    def update(running, key_block, value_block, doc_block, key_first):
        highest, totals, accum = running
        scores = (
            jnp.einsum("gqd,kgd->gqk", query_rows, key_block, preferred_element_type=jnp.float32)
            * scale
        )
        key_place = key_first + lax.broadcasted_iota(jnp.int32, (key_block.shape[0],), 0)
        allowed = (key_place[None, :] <= query_place[:, None]) & (
            doc_block[None, :] == query_docs[:, None]
        )
        masked = jnp.where(allowed[None], scores, -1e30)
        new_highest = jnp.maximum(highest, jnp.max(masked, axis=2))
        weights = jnp.where(allowed[None], jnp.exp(scores - new_highest[..., None]), 0.0)
        factor = jnp.exp(highest - new_highest)
        totals = totals * factor + jnp.sum(weights, axis=2)
        accum = accum * factor[..., None] + jnp.einsum(
            "gqk,kgd->gqd",
            weights.astype(jnp.bfloat16),
            value_block,
            preferred_element_type=jnp.float32,
        )
        return (new_highest, totals, accum)

    start_state = (
        jnp.full((groups_here, tokens_here * mixing_ratio), -1e30, jnp.float32),
        jnp.zeros((groups_here, tokens_here * mixing_ratio), jnp.float32),
        jnp.zeros((groups_here, tokens_here * mixing_ratio, head_size), jnp.float32),
    )
    key_piece = lax.all_gather(key_states, "ctx", axis=1, tiled=True)
    value_piece = lax.all_gather(values, "ctx", axis=1, tiled=True)
    doc_piece = lax.all_gather(doc_ids, "ctx", axis=1, tiled=True)
    piece_rows = key_piece.shape[1]
    block_rows = math.gcd(piece_rows, 512)

    def step(block_number, inner):
        block_offset = block_number * block_rows
        key_block = lax.dynamic_slice_in_dim(key_piece[0], block_offset, block_rows, 0)
        value_block = lax.dynamic_slice_in_dim(value_piece[0], block_offset, block_rows, 0)
        doc_block = lax.dynamic_slice_in_dim(doc_piece[0], block_offset, block_rows, 0)
        return update(inner, key_block, value_block, doc_block, block_offset)

    highest, totals, accum = lax.fori_loop(0, piece_rows // block_rows, step, start_state)
    blended_output = (accum / totals[..., None]).astype(jnp.bfloat16)
    blended_output = blended_output.reshape(
        groups_here, tokens_here, mixing_ratio, head_size
    ).transpose(1, 0, 2, 3)
    attn_rows = blended_output.reshape(pair_count, part_rows, heads_here * head_size)
    columns = out_proj.shape[1]
    gathered = lax.all_gather(attn_rows, "ctx", axis=1, tiled=True)
    gathered = gathered.reshape(pair_count * ctx_count * part_rows, heads_here * head_size)
    own_columns = lax.psum_scatter(
        jnp.dot(gathered, out_proj, preferred_element_type=jnp.float32).astype(jnp.bfloat16),
        "tp",
        scatter_dimension=0,
        tiled=True,
    ).astype(jnp.float32)
    own_columns = own_columns.reshape(ctx_count, part_rows, columns)
    projected = (
        lax.all_to_all(
            own_columns.astype(jnp.bfloat16), "ctx", split_axis=0, concat_axis=2, tiled=True
        )
        .astype(own_columns.dtype)
        .reshape(part_rows, columns * ctx_count)
    )
    hidden = residual[0].astype(jnp.float32) + projected
    power = jnp.mean(hidden * hidden, axis=1, keepdims=True)
    normed = (hidden * lax.rsqrt(power + EPSILON) * norm_gain.astype(jnp.float32)).astype(
        jnp.bfloat16
    )
    expert_count = keep_counts.shape[0]
    chosen = expert_ids[0, :, 0]
    onehot = (
        chosen[:, None] == lax.broadcasted_iota(jnp.int32, (part_rows, expert_count), 1)
    ).astype(jnp.float32)
    lower = (
        lax.broadcasted_iota(jnp.int32, (part_rows, part_rows), 0)
        > lax.broadcasted_iota(jnp.int32, (part_rows, part_rows), 1)
    ).astype(jnp.float32)
    earlier = jnp.dot(lower, onehot, preferred_element_type=jnp.float32)
    ranking = jnp.sum(onehot * earlier, axis=1)
    limits = jnp.sum(onehot * keep_counts.astype(jnp.float32)[None, :], axis=1)
    kept = ranking < limits
    target = chosen.astype(jnp.float32) * CAP + ranking
    slot_iota = lax.broadcasted_iota(jnp.int32, (expert_count * CAP, part_rows), 0).astype(
        jnp.float32
    )
    table = (slot_iota == target[None, :]) & kept[None, :]
    outgoing = jnp.dot(
        table.astype(jnp.bfloat16), normed, preferred_element_type=jnp.float32
    ).astype(jnp.bfloat16)
    exp_count = lax.axis_size("exp")
    outgoing = outgoing.reshape(exp_count, expert_count // exp_count, CAP, normed.shape[1])
    arrived = lax.all_to_all(outgoing, "exp", split_axis=0, concat_axis=0, tiled=True)
    logits = jnp.einsum("secd,de->sec", arrived, router, preferred_element_type=jnp.float32)
    return (arrived.astype(jnp.float32) * jax.nn.sigmoid(logits)[..., None]).astype(jnp.bfloat16)


def solution(mesh):
    placed = (
        P(("groups", "exp"), "ctx", "tp", None),
        P(("groups", "exp"), "ctx", "tp", None),
        P(("groups", "exp"), "ctx", "tp", None),
        P(("groups", "exp"), "ctx"),
        P(("groups", "exp"), ("ctx", "tp"), None),
        P("tp", "ctx"),
        P(),
        P(None, "exp"),
        P(("groups", "exp"), ("ctx", "tp"), None),
        P("groups"),
    )
    return jax.shard_map(
        on_device,
        mesh=mesh,
        in_specs=placed,
        out_specs=P(("groups", "ctx", "tp"), "exp", None, None),
        check_vma=False,
    )
```

profile of v0, /device:TPU:0, one launch (start us, length us, event | category | flops | bytes accessed | tf_op | source)
XLA Modules:
  0.0 172.3 jit_solution(3476322581073212627)
XLA Ops:
  6.5 12.9 %all_gather.14 = s32[1,512]{1,0:T(1,128)S(1)} all-gather(s32[1,128]{1,0:T(1,128)} %param.13), channel_id=1, replica_groups=mesh['groups'=2,'ctx'=4,'exp'=2,'tp'=2] {'ctx'}, dimensions={1}, use_global_device_ids=true | all-gather | bytes 2560 | tf_op jit(solution)/shard_map/all_gather | solution.py:73
  19.5 0.7 broadcast_in_dim.55
  20.4 0.9 copy.17
  21.3 13.9 %all_gather.16 = bf16[1,512,2,128]{3,1,2,0:T(8,128)(2,1)S(1)} all-gather(bf16[1,128,2,128]{3,1,2,0:T(8,128)(2,1)S(1)} %copy.17), channel_id=1, replica_groups=mesh['groups'=2,'ctx'=4,'exp'=2,'tp'=2] {'ctx'}, dimensions={1}, use_global_device_ids=true | all-gather | bytes 327680 | tf_op jit(solution)/shard_map/all_gather | solution.py:71
  35.2 1.3 copy.16
  36.8 0.7 select_reduce_fusion
  37.5 0.6 fusion
  38.3 14.1 %all_gather.17 = bf16[1,512,2,128]{3,1,2,0:T(8,128)(2,1)S(1)} all-gather(bf16[1,128,2,128]{3,1,2,0:T(8,128)(2,1)S(1)} %copy.19), channel_id=1, replica_groups=mesh['groups'=2,'ctx'=4,'exp'=2,'tp'=2] {'ctx'}, dimensions={1}, use_global_device_ids=true | all-gather | bytes 327680 | tf_op jit(solution)/shard_map/all_gather | solution.py:72
  52.5 1.2 fusion.18
  54.0 0.9 copy.22
  54.9 2.2 %reshape.135 = bf16[2,64,1280]{2,1,0:T(8,128)(2,1)} reshape(bf16[128,2,5,128]{3,2,1,0:T(8,128)(2,1)} %copy.22) | data formatting | bytes 655360 | tf_op jit(solution)/shard_map/reshape | solution.py:89
  57.1 30.9 %all-gather.2.cloned.1.call-done = bf16[2,256,1280]{2,1,0:T(8,128)(2,1)} async-done(((bf16[2,64,1280]{2,1,0:T(8,128)(2,1)}), bf16[2,256,1280]{2,1,0:T(8,128)(2,1)}) %all-gather.2.cloned.1.call-update) | async-done | bytes 1310736 | tf_op jit(solution)/shard_map/all_gather | solution.py:91
  88.1 4.2 %convolution_convert_fusion.1 = bf16[512,1280]{1,0:T(8,128)(2,1)} fusion(bf16[512,1280]{1,0:T(8,128)(2,1)} %bitcast.62, bf16[1280,1280]{1,0:T(8,128)(2,1)S(1)} %copy-done), kind=kOutput, calls=%fused_computation.1 | convolution fusion | flops 1678376960 | bytes 5898240 | tf_op jit(solution)/shard_map/dot_general | solution.py:94
  92.3 7.9 %reduce-scatter.2.cloned.1.call-done = bf16[256,1280]{1,0:T(8,128)(2,1)} async-done(((bf16[512,1280]{1,0:T(8,128)(2,1)}), bf16[256,1280]{1,0:T(8,128)(2,1)}) %reduce-scatter.2.cloned.1.call-update) | async-done | bytes 655376 | tf_op jit(solution)/shard_map/reduce_scatter | solution.py:93
  100.3 5.0 %all-to-all-start = ((bf16[4,64,1280]{2,1,0:T(8,128)(2,1)}), bf16[4,64,1280]{2,1,0:T(8,128)(2,1)}, u32[]{:S(2)}, u32[]{:S(2)}) async-start(bf16[4,64,1280]{2,1,0:T(8,128)(2,1)} %bitcast.55), calls=%async_computation.1 | async-start | bytes 1310720 | tf_op jit(solution)/shard_map/all_to_all | solution.py:101
  105.6 17.4 %all-to-all-done = bf16[4,64,1280]{2,1,0:T(8,128)(2,1)} async-done(((bf16[4,64,1280]{2,1,0:T(8,128)(2,1)}), bf16[4,64,1280]{2,1,0:T(8,128)(2,1)}, u32[]{:S(2)}, u32[]{:S(2)}) %all-to-all-start) | async-done | bytes 655392 | tf_op jit(solution)/shard_map/all_to_all | solution.py:101
  123.0 1.2 convert_bitcast_fusion
  124.2 0.8 copy.23
  125.3 0.8 copy-done.1
  126.4 1.6 convolution_convert_fusion
  128.0 3.9 %reshape.137 = bf16[2,32,2,5120]{3,2,1,0:T(2,128)(2,1)} reshape(bf16[128,5120]{1,0:T(8,128)(2,1)} %convolution_convert_fusion) | data formatting | bytes 2621440 | tf_op jit(solution)/shard_map/reshape | solution.py:134
  131.9 19.7 %all_to_all.14 = bf16[2,32,2,5120]{3,2,1,0:T(2,128)(2,1)S(1)} all-to-all(bf16[2,32,2,5120]{3,2,1,0:T(2,128)(2,1)} %reshape.137), channel_id=1, replica_groups=mesh['groups'=2,'ctx'=4,'exp'=2,'tp'=2] {'exp'}, dimensions={0} | all-to-all | bytes 2621440 | tf_op jit(solution)/shard_map/all_to_all | solution.py:135
  151.6 11.5 %fusion.9 = f32[32,1,2,2]{3,1,2,0:T(1,128)S(1)} fusion(bf16[2,32,2,5120]{3,2,1,0:T(2,128)(2,1)S(1)} %all_to_all.14, bf16[5120,32,1,1]{0,1,2,3:T(8,128)(2,1)S(1)} %bitcast.63), kind=kOutput, calls=%fused_computation.18 | convolution fusion | flops 1310720 | bytes 1638912 | tf_op jit(solution)/shard_map/secd,de->sec/dot_general | solution.py:136
  163.2 2.2 %multiply_convert_fusion = bf16[2,32,2,5120]{3,2,1,0:T(2,128)(2,1)} fusion(bf16[2,32,2,5120]{3,2,1,0:T(2,128)(2,1)S(1)} %all_to_all.14, f32[2,32,2]{2,1,0:T(8,128)S(1)} %fusion.34), kind=kLoop, calls=%fused_computation.2 | loop fusion | flops 1966080 | bytes 2621952 | tf_op jit(solution)/shard_map/convert_element_type | solution.py:137
  (34 shorter events, 2.0 us)
Async XLA Ops:
  6.5 81.5 %copy-start = (bf16[1280,1280]{1,0:T(8,128)(2,1)S(1)}, bf16[1280,1280]{1,0:T(8,128)(2,1)}, u32[]{:S(2)}) copy-start(bf16[1280,1280]{1,0:T(8,128)(2,1)} %param.15) | copy-start | bytes 9830404
  6.5 81.5 %all-gather.2.cloned.1.call-start = ((), (), s32[]{:S(2)}) async-start(), calls=%async_computation.3 | async-start | bytes 1638400 | tf_op jit(solution)/shard_map/all_gather | solution.py:91
  37.5 0.8 copy-start.2
  57.1 43.2 %reduce-scatter.2.cloned.1.call-start = ((), (), s32[]{:S(2)}) async-start(), calls=%async_computation.4 | async-start | bytes 1966080 | tf_op jit(solution)/shard_map/reduce_scatter | solution.py:93
  92.3 13.0 %copy-start.6 = (s32[64]{0:T(128)S(1)}, s32[64]{0:T(128)}, u32[]{:S(2)}) copy-start(s32[64]{0:T(128)} %param.19) | copy-start | bytes 772
  92.3 13.0 %copy-start.3 = (bf16[5120]{0:T(1024)(128)(2,1)S(1)}, bf16[5120]{0:T(1024)(128)(2,1)}, u32[]{:S(2)}) copy-start(bf16[5120]{0:T(1024)(128)(2,1)} %param.16) | copy-start | bytes 30724
  92.3 13.0 %copy-start.4 = (s32[1,64,1]{1,2,0:T(1,128)S(1)}, s32[1,64,1]{1,2,0:T(1,128)}, u32[]{:S(2)}) copy-start(s32[1,64,1]{1,2,0:T(1,128)} %param.18) | copy-start | bytes 772
  100.3 22.7 %all-to-all-start = ((bf16[4,64,1280]{2,1,0:T(8,128)(2,1)}), bf16[4,64,1280]{2,1,0:T(8,128)(2,1)}, u32[]{:S(2)}, u32[]{:S(2)}) async-start(bf16[4,64,1280]{2,1,0:T(8,128)(2,1)} %bitcast.55), calls=%async_computation.1 | async-start | bytes 1310720 | tf_op jit(solution)/shard_map/all_to_all | solution.py:101
  125.0 1.1 copy-start.1
  131.9 19.7 %copy-start.5 = (bf16[5120,32]{0,1:T(8,128)(2,1)S(1)}, bf16[5120,32]{0,1:T(8,128)(2,1)}, u32[]{:S(2)}) copy-start(bf16[5120,32]{0,1:T(8,128)(2,1)} %param.17) | copy-start | bytes 983044
Sparse Core Ops, SparseCore 0:
  57.2 30.8 all-gather.1
  92.4 7.7 reduce-scatter.1
where the time goes:
time: 173 us; the launch traced here: 172 us
  blocking collectives  60.6 us (35%)
  waiting for transfers between devices  56.3 us (33%)
  matrix products  19.5 us (11%)
  between operations  13.6 us (8%)
  local copies, waits for them, and re-layouts  12.5 us (7%)
  starting transfers between devices  5.02 us (3%)
  other arithmetic  4.83 us (3%)
    all_gather x1, waiting for transfers between devices, on_device(): gathered = lax.all_gather(attn_rows, 'ctx', axis=1, tiled=True)  30.9 us
    all_to_all x1, blocking collectives, on_device(): lax.all_to_all(outgoing, 'exp', split_axis=0, concat_axis=0, tiled=True)  19.7 us
    all_to_all x1, waiting for transfers between devices, on_device(): lax.all_to_all(own_columns.astype(jnp.bfloat16), 'ctx', split_axis=0, con...  17.4 us
    all_gather x1, blocking collectives, on_device(): value_piece = lax.all_gather(values, 'ctx', axis=1, tiled=True)  14.1 us
    all_gather x1, blocking collectives, on_device(): key_piece = lax.all_gather(key_states, 'ctx', axis=1, tiled=True)  13.9 us
    all_gather x1, blocking collectives, on_device(): doc_piece = lax.all_gather(doc_ids, 'ctx', axis=1, tiled=True)  12.9 us
    dot_general x1, matrix products, on_device(): jnp.einsum('secd,de->sec', arrived, router, preferred_element_type=jnp.fl...  11.5 us
    reduce_scatter x1, waiting for transfers between devices, on_device(): lax.psum_scatter(jnp.dot(gathered, out_proj, preferred_element_type=jnp.f...  7.95 us
  transfers between devices with their start and end apart: 3, of which 3 were waited for; matrix products, arithmetic and copies ran while one was open for 0% of the time, Pallas kernels for 0%

commit v1 on v0

--- a/solution.py
+++ b/solution.py
@@ -68,7 +68,26 @@
         jnp.zeros((groups_here, tokens_here * mixing_ratio), jnp.float32),
         jnp.zeros((groups_here, tokens_here * mixing_ratio, head_size), jnp.float32),
     )
-    key_piece = lax.all_gather(key_states, "ctx", axis=1, tiled=True)
+    length, index, rows = (lax.axis_size("ctx"), lax.axis_index("ctx"), key_states.shape[1])
+    upward = [(i, (i + 1) % length) for i in range(length)]
+    left = [(i, (i - 1) % length) for i in range(length)]
+    whole = jnp.zeros(
+        (*key_states.shape[:1], length * rows, *key_states.shape[1 + 1 :]), key_states.dtype
+    )
+    whole = lax.dynamic_update_slice_in_dim(whole, key_states, index * rows, axis=1)
+    from_left = from_right = key_states
+    half = length // 2
+    for step_2 in range(1, half + 1):
+        from_left = lax.ppermute(from_left, "ctx", upward)
+        whole = lax.dynamic_update_slice_in_dim(
+            whole, from_left, (index - step_2) % length * rows, axis=1
+        )
+        if step_2 < length - half:
+            from_right = lax.ppermute(from_right, "ctx", left)
+            whole = lax.dynamic_update_slice_in_dim(
+                whole, from_right, (index + step_2) % length * rows, axis=1
+            )
+    key_piece = whole
     value_piece = lax.all_gather(values, "ctx", axis=1, tiled=True)
     doc_piece = lax.all_gather(doc_ids, "ctx", axis=1, tiled=True)
     piece_rows = key_piece.shape[1]

time: 173 us -> 167 us (0.965)
  blocking collectives: 60.6 us -> 43.4 us
  waiting for transfers between devices: 56.3 us -> 62.1 us
  starting transfers between devices: 5.02 us -> 10.2 us
    all_gather x1 -> x0, blocking collectives: 13.9 us -> none  [on_device(): key_piece = lax.all_gather(key_states, 'ctx', axis=1, tiled=True)]
    ppermute x0 -> x3, waiting for transfers between devices: none -> 6.01 us  [the longest x2 6.01 us: on_device(): from_left = lax.ppermute(from_left, 'ctx', upward)]
    ppermute x0 -> x3, starting transfers between devices: none -> 5.2 us  [the longest x2 3.11 us: on_device(): from_left = lax.ppermute(from_left, 'ctx', upward)]
    all_gather x1, blocking collectives: 12.9 us -> 9.69 us  [on_device(): doc_piece = lax.all_gather(doc_ids, 'ctx', axis=1, tiled=True)]
  transfers between devices with their start and end apart: 3 -> 6, of which waited for: 3 -> 4; matrix products, arithmetic and copies ran while one was open for 0% -> 3% of each run, Pallas kernels for 0% -> 0%
where the time goes in v1:
time: 167 us
  waiting for transfers between devices  62.1 us (37%)
  blocking collectives  43.4 us (26%)
  matrix products  19.5 us (12%)
  between operations  13.6 us (8%)
  local copies, waits for them, and re-layouts  13.1 us (8%)
  starting transfers between devices  10.2 us (6%)
  other arithmetic  4.83 us (3%)
    all_gather x1, waiting for transfers between devices, on_device(): gathered = lax.all_gather(attn_rows, 'ctx', axis=1, tiled=True)  30.7 us
    all_to_all x1, blocking collectives, on_device(): lax.all_to_all(outgoing, 'exp', split_axis=0, concat_axis=0, tiled=True)  19.7 us
    all_to_all x1, waiting for transfers between devices, on_device(): lax.all_to_all(own_columns.astype(jnp.bfloat16), 'ctx', split_axis=0, con...  17.4 us
    all_gather x1, blocking collectives, on_device(): value_piece = lax.all_gather(values, 'ctx', axis=1, tiled=True)  14 us
    dot_general x1, matrix products, on_device(): jnp.einsum('secd,de->sec', arrived, router, preferred_element_type=jnp.fl...  11.5 us
    all_gather x1, blocking collectives, on_device(): doc_piece = lax.all_gather(doc_ids, 'ctx', axis=1, tiled=True)  9.69 us
    reduce_scatter x1, waiting for transfers between devices, on_device(): lax.psum_scatter(jnp.dot(gathered, out_proj, preferred_element_type=jnp.f...  7.95 us
    ppermute x2, waiting for transfers between devices, on_device(): from_left = lax.ppermute(from_left, 'ctx', upward)  6.01 us
  transfers between devices with their start and end apart: 6, of which 4 were waited for; matrix products, arithmetic and copies ran while one was open for 3% of the time, Pallas kernels for 0%

profile of v1, /device:TPU:0, one launch (start us, length us, event | category | flops | bytes accessed | tf_op | source)
XLA Modules:
  0.0 166.8 jit_solution(16915490235692272457)
XLA Ops:
  6.5 3.1 %collective-permute-start = (bf16[1,128,2,128]{3,2,1,0:T(2,128)(2,1)}, bf16[1,128,2,128]{3,2,1,0:T(2,128)(2,1)S(1)}, u32[]{:S(2)}, u32[]{:S(2)}) collective-permute-start(bf16[1,128,2,128]{3,2,1,0:T(2,128)(2,1)} %param.11), channel_id=1, source_target_pairs={{0,4},{4,8},{8,12},{12,0},{1,5},{5,9},{9,13},{13,1},{2,6},{6,10},{... | collective-permute-start | bytes 196616 | tf_op jit(solution)/shard_map/ppermute | solution.py:81
  9.6 2.1 %collective-permute-start.1 = (bf16[1,128,2,128]{3,2,1,0:T(2,128)(2,1)}, bf16[1,128,2,128]{3,2,1,0:T(2,128)(2,1)S(1)}, u32[]{:S(2)}, u32[]{:S(2)}) collective-permute-start(bf16[1,128,2,128]{3,2,1,0:T(2,128)(2,1)} %param.11), channel_id=1, source_target_pairs={{0,12},{4,0},{8,4},{12,8},{1,13},{5,1},{9,5},{13,9},{2,14},{6,2},{... | collective-permute-start | bytes 196616 | tf_op jit(solution)/shard_map/ppermute | solution.py:86
  11.7 9.7 %all_gather.11 = s32[1,512]{1,0:T(1,128)S(1)} all-gather(s32[1,128]{1,0:T(1,128)} %param.13), channel_id=1, replica_groups=mesh['groups'=2,'ctx'=4,'exp'=2,'tp'=2] {'ctx'}, dimensions={1}, use_global_device_ids=true | all-gather | bytes 2560 | tf_op jit(solution)/shard_map/all_gather | solution.py:92
  21.4 0.7 broadcast_in_dim.56
  22.3 2.0 %copy.23 = bf16[128,2,5,128]{3,1,2,0:T(2,128)(2,1)} copy(bf16[128,2,5,128]{3,0,2,1:T(8,128)(2,1)} %bitcast.76) | data formatting | bytes 655360 | tf_op jit(solution)/shard_map/reshape;squeeze | solution.py:34
  24.4 0.8 copy.25
  25.7 14.0 %all_gather.13 = bf16[1,512,2,128]{3,1,2,0:T(8,128)(2,1)S(1)} all-gather(bf16[1,128,2,128]{3,1,2,0:T(8,128)(2,1)S(1)} %copy.25), channel_id=1, replica_groups=mesh['groups'=2,'ctx'=4,'exp'=2,'tp'=2] {'ctx'}, dimensions={1}, use_global_device_ids=true | all-gather | bytes 327680 | tf_op jit(solution)/shard_map/all_gather | solution.py:91
  39.8 6.0 %collective-permute-done.2 = bf16[1,128,2,128]{3,2,1,0:T(2,128)(2,1)S(1)} collective-permute-done((bf16[1,128,2,128]{3,2,1,0:T(2,128)(2,1)S(1)}, bf16[1,128,2,128]{3,2,1,0:T(2,128)(2,1)S(1)}, u32[]{:S(2)}, u32[]{:S(2)}) %collective-permute-start.2) | collective-permute-done | bytes 65568 | tf_op jit(solution)/shard_map/ppermute | solution.py:81
  47.2 1.2 fusion.21
  48.8 0.9 copy.28
  49.7 2.1 %reshape.143 = bf16[2,64,1280]{2,1,0:T(8,128)(2,1)} reshape(bf16[128,2,5,128]{3,2,1,0:T(8,128)(2,1)} %copy.28) | data formatting | bytes 655360 | tf_op jit(solution)/shard_map/reshape | solution.py:108
  51.9 30.7 %all-gather.2.cloned.1.call-done = bf16[2,256,1280]{2,1,0:T(8,128)(2,1)} async-done(((bf16[2,64,1280]{2,1,0:T(8,128)(2,1)}), bf16[2,256,1280]{2,1,0:T(8,128)(2,1)}) %all-gather.2.cloned.1.call-update) | async-done | bytes 1310736 | tf_op jit(solution)/shard_map/all_gather | solution.py:110
  82.5 4.2 %convolution_convert_fusion.1 = bf16[512,1280]{1,0:T(8,128)(2,1)} fusion(bf16[512,1280]{1,0:T(8,128)(2,1)} %bitcast.86, bf16[1280,1280]{1,0:T(8,128)(2,1)S(1)} %copy-done), kind=kOutput, calls=%fused_computation.1 | convolution fusion | flops 1678376960 | bytes 5898240 | tf_op jit(solution)/shard_map/dot_general | solution.py:113
  86.8 7.9 %reduce-scatter.2.cloned.1.call-done = bf16[256,1280]{1,0:T(8,128)(2,1)} async-done(((bf16[512,1280]{1,0:T(8,128)(2,1)}), bf16[256,1280]{1,0:T(8,128)(2,1)}) %reduce-scatter.2.cloned.1.call-update) | async-done | bytes 655376 | tf_op jit(solution)/shard_map/reduce_scatter | solution.py:112
  94.8 5.0 %all-to-all-start = ((bf16[4,64,1280]{2,1,0:T(8,128)(2,1)}), bf16[4,64,1280]{2,1,0:T(8,128)(2,1)}, u32[]{:S(2)}, u32[]{:S(2)}) async-start(bf16[4,64,1280]{2,1,0:T(8,128)(2,1)} %bitcast.75), calls=%async_computation.1 | async-start | bytes 1310720 | tf_op jit(solution)/shard_map/all_to_all | solution.py:120
  100.0 17.4 %all-to-all-done = bf16[4,64,1280]{2,1,0:T(8,128)(2,1)} async-done(((bf16[4,64,1280]{2,1,0:T(8,128)(2,1)}), bf16[4,64,1280]{2,1,0:T(8,128)(2,1)}, u32[]{:S(2)}, u32[]{:S(2)}) %all-to-all-start) | async-done | bytes 655392 | tf_op jit(solution)/shard_map/all_to_all | solution.py:120
  117.5 1.2 convert_bitcast_fusion
  118.6 0.8 copy.29
  119.8 0.8 copy-done.1
  120.9 1.6 convolution_convert_fusion
  122.5 3.9 %reshape.145 = bf16[2,32,2,5120]{3,2,1,0:T(2,128)(2,1)} reshape(bf16[128,5120]{1,0:T(8,128)(2,1)} %convolution_convert_fusion) | data formatting | bytes 2621440 | tf_op jit(solution)/shard_map/reshape | solution.py:153
  126.4 19.7 %all_to_all.14 = bf16[2,32,2,5120]{3,2,1,0:T(2,128)(2,1)S(1)} all-to-all(bf16[2,32,2,5120]{3,2,1,0:T(2,128)(2,1)} %reshape.145), channel_id=1, replica_groups=mesh['groups'=2,'ctx'=4,'exp'=2,'tp'=2] {'exp'}, dimensions={0} | all-to-all | bytes 2621440 | tf_op jit(solution)/shard_map/all_to_all | solution.py:154
  146.1 11.5 %fusion.12 = f32[32,1,2,2]{3,1,2,0:T(1,128)S(1)} fusion(bf16[2,32,2,5120]{3,2,1,0:T(2,128)(2,1)S(1)} %all_to_all.14, bf16[5120,32,1,1]{0,1,2,3:T(8,128)(2,1)S(1)} %bitcast.87), kind=kOutput, calls=%fused_computation.21 | convolution fusion | flops 1310720 | bytes 1638912 | tf_op jit(solution)/shard_map/secd,de->sec/dot_general | solution.py:155
  157.7 2.2 %multiply_convert_fusion = bf16[2,32,2,5120]{3,2,1,0:T(2,128)(2,1)} fusion(bf16[2,32,2,5120]{3,2,1,0:T(2,128)(2,1)S(1)} %all_to_all.14, f32[2,32,2]{2,1,0:T(8,128)S(1)} %fusion.36), kind=kLoop, calls=%fused_computation.7 | loop fusion | flops 1966080 | bytes 2621952 | tf_op jit(solution)/shard_map/convert_element_type | solution.py:156
  (45 shorter events, 3.3 us)
Async XLA Ops:
  6.5 76.0 %copy-start = (bf16[1280,1280]{1,0:T(8,128)(2,1)S(1)}, bf16[1280,1280]{1,0:T(8,128)(2,1)}, u32[]{:S(2)}) copy-start(bf16[1280,1280]{1,0:T(8,128)(2,1)} %param.15) | copy-start | bytes 9830404
  6.5 18.8 %copy-start.3 = (bf16[1,128,2,128]{3,2,1,0:T(2,128)(2,1)S(1)}, bf16[1,128,2,128]{3,2,1,0:T(2,128)(2,1)}, u32[]{:S(2)}) copy-start(bf16[1,128,2,128]{3,2,1,0:T(2,128)(2,1)} %param.11) | copy-start | bytes 196612
  6.5 76.0 %all-gather.2.cloned.1.call-start = ((), (), s32[]{:S(2)}) async-start(), calls=%async_computation.3 | async-start | bytes 1638400 | tf_op jit(solution)/shard_map/all_gather | solution.py:110
  6.5 33.2 %collective-permute-start = (bf16[1,128,2,128]{3,2,1,0:T(2,128)(2,1)}, bf16[1,128,2,128]{3,2,1,0:T(2,128)(2,1)S(1)}, u32[]{:S(2)}, u32[]{:S(2)}) collective-permute-start(bf16[1,128,2,128]{3,2,1,0:T(2,128)(2,1)} %param.11), channel_id=1, source_target_pairs={{0,4},{4,8},{8,12},{12,0},{1,5},{5,9},{9,13},{13,1},{2,6},{6,10},{... | collective-permute-start | bytes 196616 | tf_op jit(solution)/shard_map/ppermute | solution.py:81
  9.6 30.2 %collective-permute-start.1 = (bf16[1,128,2,128]{3,2,1,0:T(2,128)(2,1)}, bf16[1,128,2,128]{3,2,1,0:T(2,128)(2,1)S(1)}, u32[]{:S(2)}, u32[]{:S(2)}) collective-permute-start(bf16[1,128,2,128]{3,2,1,0:T(2,128)(2,1)} %param.11), channel_id=1, source_target_pairs={{0,12},{4,0},{8,4},{12,8},{1,13},{5,1},{9,5},{13,9},{2,14},{6,2},{... | collective-permute-start | bytes 196616 | tf_op jit(solution)/shard_map/ppermute | solution.py:86
  25.2 20.6 %copy-start.2 = (bf16[128,2,5,128]{3,1,2,0:T(2,128)(2,1)S(1)}, bf16[128,2,5,128]{3,1,2,0:T(2,128)(2,1)}, u32[]{:S(2)}) copy-start(bf16[128,2,5,128]{3,1,2,0:T(2,128)(2,1)} %copy.23) | copy-start | bytes 983044
  39.7 6.1 %collective-permute-start.2 = (bf16[1,128,2,128]{3,2,1,0:T(2,128)(2,1)S(1)}, bf16[1,128,2,128]{3,2,1,0:T(2,128)(2,1)S(1)}, u32[]{:S(2)}, u32[]{:S(2)}) collective-permute-start(bf16[1,128,2,128]{3,2,1,0:T(2,128)(2,1)S(1)} %collective-permute-done), channel_id=1, source_target_pairs={{0,4},{4,8},{8,12},{12,0},{1,5},{5,9},{9,13},{13,1},{2,6},{6,10},{... | collective-permute-start | bytes 196616 | tf_op jit(solution)/shard_map/ppermute | solution.py:81
  51.8 42.9 %reduce-scatter.2.cloned.1.call-start = ((), (), s32[]{:S(2)}) async-start(), calls=%async_computation.4 | async-start | bytes 1966080 | tf_op jit(solution)/shard_map/reduce_scatter | solution.py:112
  86.8 13.0 %copy-start.7 = (s32[64]{0:T(128)S(1)}, s32[64]{0:T(128)}, u32[]{:S(2)}) copy-start(s32[64]{0:T(128)} %param.19) | copy-start | bytes 772
  86.8 13.0 %copy-start.4 = (bf16[5120]{0:T(1024)(128)(2,1)S(1)}, bf16[5120]{0:T(1024)(128)(2,1)}, u32[]{:S(2)}) copy-start(bf16[5120]{0:T(1024)(128)(2,1)} %param.16) | copy-start | bytes 30724
  86.8 13.0 %copy-start.5 = (s32[1,64,1]{1,2,0:T(1,128)S(1)}, s32[1,64,1]{1,2,0:T(1,128)}, u32[]{:S(2)}) copy-start(s32[1,64,1]{1,2,0:T(1,128)} %param.18) | copy-start | bytes 772
  94.8 22.7 %all-to-all-start = ((bf16[4,64,1280]{2,1,0:T(8,128)(2,1)}), bf16[4,64,1280]{2,1,0:T(8,128)(2,1)}, u32[]{:S(2)}, u32[]{:S(2)}) async-start(bf16[4,64,1280]{2,1,0:T(8,128)(2,1)} %bitcast.75), calls=%async_computation.1 | async-start | bytes 1310720 | tf_op jit(solution)/shard_map/all_to_all | solution.py:120
  119.5 1.1 copy-start.1
  126.4 19.7 %copy-start.6 = (bf16[5120,32]{0,1:T(8,128)(2,1)S(1)}, bf16[5120,32]{0,1:T(8,128)(2,1)}, u32[]{:S(2)}) copy-start(bf16[5120,32]{0,1:T(8,128)(2,1)} %param.17) | copy-start | bytes 983044
Sparse Core Ops, SparseCore 0:
  52.0 30.5 all-gather.1
  86.9 7.7 reduce-scatter.1
